TPU v7x, 256 devices: a whole 4x4x8 slice. The times are simulated.
256 devices in a mesh: head: 8 (over y, x_lo), seq: 32 (over z, x_hi, core).
Axes of the slice: x: 4 (x_hi: 2, x_lo: 2; x = x_hi * 2 + x_lo), y: 4, z: 8, core: 2. Of those that a mesh axis runs over, the one named last changes fastest.
Arguments:
- query: bfloat16 [32768, 3072], P(('seq', 'head')), may hold values from -9 to 9
- key: bfloat16 [32768, 3072], P(('seq', 'head')), may hold values from -9 to 9
- value: bfloat16 [32768, 3072], P(('seq', 'head')), may hold values from -6 to 6
- grad_out: bfloat16 [32768, 3072], P(('seq', 'head')), may hold values from -6 to 6
- tile_list: int32 [256, 12], replicated, may hold values from 0 to 255, as said below
- tile_count: int32 [256], replicated, may hold values from 1 to 12, as said below
Outputs:
- attn_out: bfloat16 [32768, 3072], P(('seq', 'head'))
- grad_query: bfloat16 [32768, 3072], P(('seq', 'head'))
- grad_key: bfloat16 [32768, 3072], P(('seq', 'head'))
- grad_value: bfloat16 [32768, 3072], P(('seq', 'head'))
Inputs may be any that keep to these rules, and one draw needn't show every extreme that they name: `tile_list`: tile g sits at frame block g // 8, tile row (g // 2) % 4 and tile column g % 2. Row a lists only tiles at most one step from tile a along each of the three tile axes; its first entry is a itself; its first tile_count[a] entries are distinct; entries from tile_count[a] on are to be ignored. `tile_count`: the number of used entries of each row of tile_list.
All inputs are finite; a program needn't handle non-finite values.
Results may differ from a plain program's by a relative error of at most 0.012.
The roundings to bfloat16 on the way count: a program that leaves them out, or rounds other values in their place, can miss the bound.
Values may be sent and summed in bfloat16 or wider, within the bound.
A program may use at most 128 MiB of HBM per device.

v0:
```python
import jax
import jax.numpy as jnp
from jax import lax
from jax.sharding import PartitionSpec as P

HD = 128
TILE = 128
TILES_DEV = 8
SLAB = 1024


def padded(cells, sides, width):
    for axis, dim in sides:
        count = lax.axis_size(axis)
        ends = count - 1
        head = lax.slice_in_dim(cells, 0, width, axis=dim)
        tail = lax.slice_in_dim(cells, cells.shape[dim] - width, cells.shape[dim], axis=dim)
        cells = jnp.concatenate(
            [
                lax.ppermute(tail, axis, [(i, (i + 1) % count) for i in range(ends)]),
                cells,
                lax.ppermute(head, axis, [((i + 1) % count, i) for i in range(ends)]),
            ],
            axis=dim,
        )
    return cells


def passed_along(block, axis, distance):
    devices = range(lax.axis_size(axis))
    route = [(i - distance, i) for i in devices if i - distance in devices]
    return lax.ppermute(block, axis, route)


def tile_scores(query_tiles, key_tiles, scaling):
    return (
        jnp.einsum("tqhd,tkhd->thqk", query_tiles, key_tiles, preferred_element_type=jnp.float32)
        * scaling
    )


def selector(slots, width, dtype):
    return (slots[:, None] == jnp.arange(width, dtype=jnp.int32)[None, :]).astype(dtype)


def pick_tiles(pool, slots):
    chooser = selector(slots, pool.shape[0], pool.dtype)
    picked = jnp.einsum("tp,pkhd->tkhd", chooser, pool, preferred_element_type=jnp.float32)
    return picked.astype(pool.dtype)


def spread_tiles(values, slots, width):
    chooser = selector(slots, width, jnp.float32)
    return jnp.einsum("tp,tkhd->pkhd", chooser, values, precision=lax.Precision.HIGHEST)


def tile_grads(
    query_tiles, cotangent_tiles, key_tiles, value_tiles, log_total, row_delta, in_use, scaling
):
    score = tile_scores(query_tiles, key_tiles, scaling)
    probability = jnp.where(in_use, jnp.exp(score - log_total[..., None]), 0.0)
    prob_b = probability.astype(jnp.bfloat16)
    grad_prob = jnp.einsum(
        "tqhd,tkhd->thqk", cotangent_tiles, value_tiles, preferred_element_type=jnp.float32
    )
    grad_score = (probability * (grad_prob - row_delta[..., None])).astype(jnp.bfloat16)
    key_grad = jnp.einsum(
        "thqk,tqhd->tkhd", grad_score, query_tiles, preferred_element_type=jnp.float32
    )
    value_grad = jnp.einsum(
        "thqk,tqhd->tkhd", prob_b, cotangent_tiles, preferred_element_type=jnp.float32
    )
    return (grad_score, key_grad, value_grad)


def per_device(query, key, value, grad_out, tile_list, tile_count):
    scaling = HD ** (-0.5)
    slab_index = lax.axis_index("seq")
    query_heads, key_heads, value_heads, cotangent_heads = (
        lax.all_to_all(query, "head", split_axis=1, concat_axis=0, tiled=True),
        lax.all_to_all(key, "head", split_axis=1, concat_axis=0, tiled=True),
        lax.all_to_all(value, "head", split_axis=1, concat_axis=0, tiled=True),
        lax.all_to_all(grad_out, "head", split_axis=1, concat_axis=0, tiled=True),
    )
    columns = query_heads.shape[1]
    heads_dev = columns // HD
    tile_shape = (TILES_DEV, TILE, heads_dev, HD)
    query_tiles = query_heads.reshape(tile_shape)
    key_value = jnp.stack([key_heads, value_heads])
    with_rims = padded(key_value, (("seq", 1),), SLAB)
    kv_pool = with_rims.reshape(2, 3 * TILES_DEV, TILE, heads_dev, HD)
    keys_pool = kv_pool[0]
    values_pool = kv_pool[1]
    pool_width = 3 * TILES_DEV
    own_list = lax.dynamic_slice_in_dim(tile_list, slab_index * TILES_DEV, TILES_DEV, 0)
    own_count = lax.dynamic_slice_in_dim(tile_count, slab_index * TILES_DEV, TILES_DEV, 0)
    pool_slots = (own_list // TILES_DEV - slab_index + 1) * TILES_DEV + own_list % TILES_DEV
    busiest = jnp.max(own_count)

    def norm_pass(slot_index, running):
        running_max, row_total = running
        picked = lax.dynamic_index_in_dim(pool_slots, slot_index, 1, keepdims=False)
        score = tile_scores(query_tiles, pick_tiles(keys_pool, picked), scaling)
        in_use = (slot_index < own_count)[:, None, None]
        new_max = jnp.where(in_use, jnp.maximum(running_max, jnp.max(score, axis=3)), running_max)
        added = jnp.where(in_use, jnp.sum(jnp.exp(score - new_max[..., None]), axis=3), 0.0)
        return (new_max, row_total * jnp.exp(running_max - new_max) + added)

    stat_shape = (TILES_DEV, heads_dev, TILE)
    running_max, row_total = lax.fori_loop(
        0,
        busiest,
        norm_pass,
        (jnp.full(stat_shape, -jnp.inf, jnp.float32), jnp.zeros(stat_shape, jnp.float32)),
    )
    log_total = running_max + jnp.log(row_total)

    def value_pass(slot_index, accum):
        picked = lax.dynamic_index_in_dim(pool_slots, slot_index, 1, keepdims=False)
        score = tile_scores(query_tiles, pick_tiles(keys_pool, picked), scaling)
        in_use = (slot_index < own_count)[:, None, None, None]
        prob_b = jnp.where(in_use, jnp.exp(score - log_total[..., None]), 0.0).astype(jnp.bfloat16)
        return accum + jnp.einsum(
            "thqk,tkhd->tqhd",
            prob_b,
            pick_tiles(values_pool, picked),
            preferred_element_type=jnp.float32,
        )

    attn_tiles = lax.fori_loop(0, busiest, value_pass, jnp.zeros(tile_shape, jnp.float32)).astype(
        jnp.bfloat16
    )
    attn_heads = attn_tiles.reshape(SLAB, columns)
    attn_out = lax.all_to_all(attn_heads, "head", split_axis=0, concat_axis=1, tiled=True)
    cotangent_tiles = cotangent_heads.reshape(tile_shape)
    attn_wide = lax.optimization_barrier(attn_tiles).astype(jnp.float32)
    row_delta = jnp.transpose(
        jnp.sum(cotangent_tiles.astype(jnp.float32) * attn_wide, axis=3), (0, 2, 1)
    )

    def backward_pass(slot_index, carried):
        grad_accum, pool_key, pool_value = carried
        picked = lax.dynamic_index_in_dim(pool_slots, slot_index, 1, keepdims=False)
        key_tiles = pick_tiles(keys_pool, picked)
        in_use = (slot_index < own_count)[:, None, None, None]
        grad_score, key_grad, value_grad = tile_grads(
            query_tiles,
            cotangent_tiles,
            key_tiles,
            pick_tiles(values_pool, picked),
            log_total,
            row_delta,
            in_use,
            scaling,
        )
        grad_accum = grad_accum + jnp.einsum(
            "thqk,tkhd->tqhd", grad_score, key_tiles, preferred_element_type=jnp.float32
        )
        pool_key = pool_key + spread_tiles(key_grad, picked, pool_width)
        pool_value = pool_value + spread_tiles(value_grad, picked, pool_width)
        return (grad_accum, pool_key, pool_value)

    empty_pool = jnp.zeros((pool_width,) + tile_shape[1:], jnp.float32)
    grad_accum, pool_key, pool_value = lax.fori_loop(
        0, busiest, backward_pass, (jnp.zeros(tile_shape, jnp.float32), empty_pool, empty_pool)
    )
    own_key = pool_key[TILES_DEV : 2 * TILES_DEV]
    own_value = pool_value[TILES_DEV : 2 * TILES_DEV]
    lower_part = jnp.stack([pool_key[:TILES_DEV], pool_value[:TILES_DEV]]).astype(jnp.bfloat16)
    upper_part = jnp.stack([pool_key[2 * TILES_DEV :], pool_value[2 * TILES_DEV :]]).astype(
        jnp.bfloat16
    )
    from_below = passed_along(upper_part, "seq", 1).astype(jnp.float32)
    from_above = passed_along(lower_part, "seq", -1).astype(jnp.float32)
    grad_key_sum = own_key + from_below[0] + from_above[0]
    grad_value_sum = own_value + from_below[1] + from_above[1]
    query_grad = (scaling * grad_accum).astype(jnp.bfloat16).reshape(SLAB, columns)
    key_grad_out = (scaling * grad_key_sum).astype(jnp.bfloat16).reshape(SLAB, columns)
    value_grad_out = grad_value_sum.astype(jnp.bfloat16).reshape(SLAB, columns)
    grad_query, grad_key, grad_value = (
        lax.all_to_all(query_grad, "head", split_axis=0, concat_axis=1, tiled=True),
        lax.all_to_all(key_grad_out, "head", split_axis=0, concat_axis=1, tiled=True),
        lax.all_to_all(value_grad_out, "head", split_axis=0, concat_axis=1, tiled=True),
    )
    return (attn_out, grad_query, grad_key, grad_value)


def solution(mesh):
    placed = (
        P(("seq", "head"), None),
        P(("seq", "head"), None),
        P(("seq", "head"), None),
        P(("seq", "head"), None),
        P(),
        P(),
    )
    return jax.shard_map(
        per_device,
        mesh=mesh,
        in_specs=placed,
        out_specs=(
            P(("seq", "head"), None),
            P(("seq", "head"), None),
            P(("seq", "head"), None),
            P(("seq", "head"), None),
        ),
        check_vma=False,
    )
```

profile of v0, /device:TPU:1, one launch (start us, length us, event | category | flops | bytes accessed | tf_op | source)
XLA Modules:
  0.0 647.6 jit_solution(8043777818952585101)
XLA Ops:
  3.3 5.9 all-to-all-start
  10.8 10.1 %all-to-all-done = bf16[128,8,384]{2,0,1:T(8,128)(2,1)S(1)} async-done(((bf16[128,8,384]{2,0,1:T(8,128)(2,1)}), bf16[128,8,384]{2,0,1:T(8,128)(2,1)S(1)}, u32[]{:S(2)}, u32[]{:S(2)}) %all-to-all-start) | async-done | bytes 786464 | tf_op jit(solution)/shard_map/all_to_all | solution.py:81
  25.0 10.9 %all-to-all-done.1 = bf16[128,8,384]{2,0,1:T(8,128)(2,1)S(1)} async-done(((bf16[128,8,384]{2,0,1:T(8,128)(2,1)}), bf16[128,8,384]{2,0,1:T(8,128)(2,1)S(1)}, u32[]{:S(2)}, u32[]{:S(2)}) %all-to-all-start.1) | async-done | bytes 786464 | tf_op jit(solution)/shard_map/all_to_all | solution.py:82
  37.5 4.8 collective-permute-start.1
  42.3 4.3 collective-permute-start
  52.5 39.9 %all-to-all-done.2 = bf16[128,8,384]{0,2,1:T(8,128)(2,1)S(1)} async-done(((bf16[128,8,384]{0,2,1:T(8,128)(2,1)}), bf16[128,8,384]{0,2,1:T(8,128)(2,1)S(1)}, u32[]{:S(2)}, u32[]{:S(2)}) %all-to-all-start.2) | async-done | bytes 786464 | tf_op jit(solution)/shard_map/all_to_all | solution.py:80
  98.3 6.6 %all-to-all-done.4 = bf16[128,8,384]{0,2,1:T(8,128)(2,1)S(1)} async-done(((bf16[128,8,384]{0,2,1:T(8,128)(2,1)}), bf16[128,8,384]{0,2,1:T(8,128)(2,1)S(1)}, u32[]{:S(2)}, u32[]{:S(2)}) %all-to-all-start.4) | async-done | bytes 786464 | tf_op jit(solution)/shard_map/all_to_all | solution.py:83
  115.7 28.3 %while.36 = (s32[]{:T(128)}, f32[8,3,128]{2,1,0:T(4,128)S(1)}, f32[8,3,128]{2,1,0:T(4,128)S(1)}, s32[]{:T(128)}, s32[8]{0:T(128)S(1)}, /*index=5*/s32[8,12]{0,1:...) while((s32[]{:T(128)}, f32[8,3,128]{2,1,0:T(4,128)S(1)}, ...), condition=%wide.region_4.5_spmd, body=%wide.region_1.4_spmd.sunk | while | flops 121516232 | bytes 8024375 | solution.py:110
  147.7 4.7 copy.79
  153.8 96.1 %while.37 = (s32[]{:T(128)}, f32[8,128,3,128]{1,3,2,0:T(8,128)}, s32[]{:T(128)}, s32[8,12]{0,1:T(8,128)S(1)}, bf16[24,128,3,128]{3,0,2,1:T(8,128)(2,1)}, /*index...) while((s32[]{:T(128)}, f32[8,128,3,128]{1,3,2,0:T(8,128)}, ...), condition=%wide.region_6.7_spmd, body=%wide.region_5.6_spmd.sunk | while | flops 241828240 | bytes 21246324 | solution.py:130
  165.7 4.0 bitcast_add_fusion.4
  173.7 4.0 bitcast_add_fusion.4
  189.6 4.0 bitcast_add_fusion.4
  197.6 4.0 bitcast_add_fusion.4
  213.5 4.0 bitcast_add_fusion.4
  221.5 4.0 bitcast_add_fusion.4
  245.4 4.0 bitcast_add_fusion.4
  260.2 285.3 %while.38 = (s32[]{:T(128)}, f32[8,128,3,128]{1,3,2,0:T(8,128)}, f32[24,128,3,128]{3,0,2,1:T(8,128)}, f32[24,128,3,128]{3,0,2,1:T(8,128)}, s32[]{:T(128)}, /*ind...) while((s32[]{:T(128)}, f32[8,128,3,128]{1,3,2,0:T(8,128)}, ...), condition=%wide.region_9.10_spmd, body=%wide.region_8.9_spmd.sunk | while | flops 773849856 | bytes 136864496 | solution.py:164
  273.3 4.3 convolution_add_fusion.4
  277.6 4.3 convolution_add_fusion.5
  297.0 4.3 convolution_add_fusion.4
  301.3 4.3 convolution_add_fusion.5
  320.6 4.3 convolution_add_fusion.4
  325.0 4.3 convolution_add_fusion.5
  344.3 4.3 convolution_add_fusion.4
  348.7 4.3 convolution_add_fusion.5
  368.0 4.3 convolution_add_fusion.4
  372.4 4.3 convolution_add_fusion.5
  391.7 4.3 convolution_add_fusion.4
  396.1 4.3 convolution_add_fusion.5
  415.4 4.3 convolution_add_fusion.4
  419.8 4.3 convolution_add_fusion.5
  439.1 4.3 convolution_add_fusion.4
  443.5 4.3 convolution_add_fusion.5
  462.8 4.3 convolution_add_fusion.4
  467.2 4.3 convolution_add_fusion.5
  486.5 4.3 convolution_add_fusion.4
  490.9 4.3 convolution_add_fusion.5
  510.2 4.3 convolution_add_fusion.4
  514.6 4.3 convolution_add_fusion.5
  533.9 4.3 convolution_add_fusion.4
  538.3 4.3 convolution_add_fusion.5
  545.5 6.1 copy.91
  554.4 6.1 copy.89
  568.1 5.3 collective-permute-start.2
  578.3 25.4 %all-to-all-done.3 = bf16[8,128,384]{1,2,0:T(8,128)(2,1)S(1)} async-done(((bf16[8,128,384]{1,2,0:T(8,128)(2,1)}), bf16[8,128,384]{1,2,0:T(8,128)(2,1)S(1)}, u32[]{:S(2)}, u32[]{:S(2)}) %all-to-all-start.3) | async-done | bytes 786464 | tf_op jit(solution)/shard_map/all_to_all | solution.py:134
  603.7 4.2 all-to-all-start.5
  624.1 9.5 %all-to-all-done.6 = bf16[8,128,384]{2,1,0:T(8,128)(2,1)S(1)} async-done(((bf16[8,128,384]{2,1,0:T(8,128)(2,1)}), bf16[8,128,384]{2,1,0:T(8,128)(2,1)S(1)}, u32[]{:S(2)}, u32[]{:S(2)}) %all-to-all-start.6) | async-done | bytes 786464 | tf_op jit(solution)/shard_map/all_to_all | solution.py:182
  (664 shorter events, 346.2 us)
Async XLA Ops:
  2.1 7.1 %copy-start.15 = (bf16[128,3072]{1,0:T(8,128)(2,1)S(1)}, bf16[128,3072]{1,0:T(8,128)(2,1)}, u32[]{:S(2)}) copy-start(bf16[128,3072]{1,0:T(8,128)(2,1)} %param.14) | copy-start | bytes 2359300
  3.3 17.6 %all-to-all-start = ((bf16[128,8,384]{2,0,1:T(8,128)(2,1)}), bf16[128,8,384]{2,0,1:T(8,128)(2,1)S(1)}, u32[]{:S(2)}, u32[]{:S(2)}) async-start(bf16[128,8,384]{2,0,1:T(8,128)(2,1)} %copy.71), calls=%async_computation | async-start | bytes 1572864 | tf_op jit(solution)/shard_map/all_to_all | solution.py:81
  20.9 15.0 %all-to-all-start.1 = ((bf16[128,8,384]{2,0,1:T(8,128)(2,1)}), bf16[128,8,384]{2,0,1:T(8,128)(2,1)S(1)}, u32[]{:S(2)}, u32[]{:S(2)}) async-start(bf16[128,8,384]{2,0,1:T(8,128)(2,1)} %copy.73), calls=%async_computation.1 | async-start | bytes 1572864 | tf_op jit(solution)/shard_map/all_to_all | solution.py:82
  36.2 10.4 %copy-start.16 = (bf16[128,3072]{1,0:T(8,128)(2,1)S(1)}, bf16[128,3072]{1,0:T(8,128)(2,1)}, u32[]{:S(2)}) copy-start(bf16[128,3072]{1,0:T(8,128)(2,1)} %param.12) | copy-start | bytes 2359300
  37.5 13.8 %copy-start.17 = (bf16[128,3072]{1,0:T(8,128)(2,1)S(1)}, bf16[128,3072]{1,0:T(8,128)(2,1)}, u32[]{:S(2)}) copy-start(bf16[128,3072]{1,0:T(8,128)(2,1)} %param.15) | copy-start | bytes 2359300
  37.5 68.6 %collective-permute-start.1 = (bf16[2,1024,384]{1,2,0:T(8,128)(2,1)}, bf16[2,1024,384]{1,2,0:T(8,128)(2,1)}, u32[]{:S(2)}, u32[]{:S(2)}) collective-permute-start(bf16[2,1024,384]{1,2,0:T(8,128)(2,1)} %pad_maximum_fusion.1), channel_id=1, source_target_pairs={{1,0},{2,1},{3,2},{4,3},{5,4},{6,5},{7,6},{8,7},{9,8},{10,9},{11,1... | collective-permute-start | bytes 4718600 | tf_op jit(solution)/shard_map/ppermute | solution.py:22
  42.3 63.8 %collective-permute-start = (bf16[2,1024,384]{1,2,0:T(8,128)(2,1)}, bf16[2,1024,384]{1,2,0:T(8,128)(2,1)}, u32[]{:S(2)}, u32[]{:S(2)}) collective-permute-start(bf16[2,1024,384]{1,2,0:T(8,128)(2,1)} %pad_maximum_fusion.1), channel_id=1, source_target_pairs={{0,1},{1,2},{2,3},{3,4},{4,5},{5,6},{6,7},{7,8},{8,9},{9,10},{10,1... | collective-permute-start | bytes 4718600 | tf_op jit(solution)/shard_map/ppermute | solution.py:20
  47.8 44.7 %all-to-all-start.2 = ((bf16[128,8,384]{0,2,1:T(8,128)(2,1)}), bf16[128,8,384]{0,2,1:T(8,128)(2,1)S(1)}, u32[]{:S(2)}, u32[]{:S(2)}) async-start(bf16[128,8,384]{0,2,1:T(8,128)(2,1)} %bitcast.22), calls=%async_computation.2 | async-start | bytes 1572864 | tf_op jit(solution)/shard_map/all_to_all | solution.py:80
  51.3 44.7 %copy-start.19 = (s32[256]{0:T(256)S(1)}, s32[256]{0:T(256)}, u32[]{:S(2)}) copy-start(s32[256]{0:T(256)} %param.17) | copy-start | bytes 3076
  51.3 45.4 %copy-start.18 = (s32[256,12]{0,1:T(8,128)S(1)}, s32[256,12]{0,1:T(8,128)}, u32[]{:S(2)}) copy-start(s32[256,12]{0,1:T(8,128)} %param.16) | copy-start | bytes 36868
  92.5 4.3 copy-start.13
  92.5 12.5 %all-to-all-start.4 = ((bf16[128,8,384]{0,2,1:T(8,128)(2,1)}), bf16[128,8,384]{0,2,1:T(8,128)(2,1)S(1)}, u32[]{:S(2)}, u32[]{:S(2)}) async-start(bf16[128,8,384]{0,2,1:T(8,128)(2,1)} %bitcast.208), calls=%async_computation.4 | async-start | bytes 1572864 | tf_op jit(solution)/shard_map/all_to_all | solution.py:83
  272.1 5.5 slice-start
  273.2 4.3 slice-start.1
  277.6 4.3 copy-start.2
  295.8 5.5 slice-start
  296.9 4.3 slice-start.1
  301.3 4.3 copy-start.2
  319.5 5.5 slice-start
  320.6 4.3 slice-start.1
  343.2 5.5 slice-start
  344.3 4.3 slice-start.1
  366.9 5.5 slice-start
  368.0 4.3 slice-start.1
  390.6 5.5 slice-start
  391.7 4.3 slice-start.1
  414.3 5.5 slice-start
  415.4 4.3 slice-start.1
  438.0 5.5 slice-start
  439.1 4.3 slice-start.1
  461.6 5.5 slice-start
  462.8 4.3 slice-start.1
  485.3 5.5 slice-start
  486.5 4.3 slice-start.1
  509.0 5.5 slice-start
  510.2 4.3 slice-start.1
  532.7 5.5 slice-start
  533.9 4.3 slice-start.1
  538.3 4.3 copy-start.2
  564.8 43.1 %collective-permute-start.3 = (bf16[2,8,128,3,128]{2,4,3,1,0:T(8,128)(2,1)}, bf16[2,8,128,3,128]{2,4,3,1,0:T(8,128)(2,1)}, u32[]{:S(2)}, u32[]{:S(2)}) collective-permute-start(bf16[2,8,128,3,128]{2,4,3,1,0:T(8,128)(2,1)} %pad_maximum_fusion.3), channel_id=1, source_target_pairs={{1,0},{2,1},{3,2},{4,3},{5,4},{6,5},{7,6},{8,7},{9,8},{10,9},{11,1... | collective-permute-start | bytes 4718600 | tf_op jit(solution)/shard_map/ppermute | solution.py:32
  568.1 8.8 %copy-start.8 = (f32[8,128,3,128]{1,3,2,0:T(8,128)S(1)}, f32[8,128,3,128]{1,3,2,0:T(8,128)}, u32[]{:S(2)}) copy-start(f32[8,128,3,128]{1,3,2,0:T(8,128)} %get-tuple-element.169) | copy-start | bytes 4718596
  568.1 41.7 %collective-permute-start.2 = (bf16[2,8,128,3,128]{2,4,3,1,0:T(8,128)(2,1)}, bf16[2,8,128,3,128]{2,4,3,1,0:T(8,128)(2,1)}, u32[]{:S(2)}, u32[]{:S(2)}) collective-permute-start(bf16[2,8,128,3,128]{2,4,3,1,0:T(8,128)(2,1)} %pad_maximum_fusion.2), channel_id=1, source_target_pairs={{0,1},{1,2},{2,3},{3,4},{4,5},{5,6},{6,7},{7,8},{8,9},{9,10},{10,1... | collective-permute-start | bytes 4718600 | tf_op jit(solution)/shard_map/ppermute | solution.py:32
  573.3 30.3 %all-to-all-start.3 = ((bf16[8,128,384]{1,2,0:T(8,128)(2,1)}), bf16[8,128,384]{1,2,0:T(8,128)(2,1)S(1)}, u32[]{:S(2)}, u32[]{:S(2)}) async-start(bf16[8,128,384]{1,2,0:T(8,128)(2,1)} %bitcast.26), calls=%async_computation.3 | async-start | bytes 1572864 | tf_op jit(solution)/shard_map/all_to_all | solution.py:134
  603.7 15.3 %all-to-all-start.5 = ((bf16[8,128,384]{2,1,0:T(8,128)(2,1)}), bf16[8,128,384]{2,1,0:T(8,128)(2,1)}, u32[]{:S(2)}, u32[]{:S(2)}) async-start(bf16[8,128,384]{2,1,0:T(8,128)(2,1)} %copy.87), calls=%async_computation.5 | async-start | bytes 1572864 | tf_op jit(solution)/shard_map/all_to_all | solution.py:181
  615.5 7.4 %copy-start.14 = (bf16[8,128,3,128]{1,3,2,0:T(8,128)(2,1)S(1)}, bf16[8,128,3,128]{1,3,2,0:T(8,128)(2,1)}, u32[]{:S(2)}) copy-start(bf16[8,128,3,128]{1,3,2,0:T(8,128)(2,1)} %get-tuple-element.355) | copy-start | bytes 2359300
  618.9 14.6 %all-to-all-start.6 = ((bf16[8,128,384]{2,1,0:T(8,128)(2,1)}), bf16[8,128,384]{2,1,0:T(8,128)(2,1)S(1)}, u32[]{:S(2)}, u32[]{:S(2)}) async-start(bf16[8,128,384]{2,1,0:T(8,128)(2,1)} %copy.92), calls=%async_computation.6 | async-start | bytes 1572864 | tf_op jit(solution)/shard_map/all_to_all | solution.py:182
  622.9 14.2 %copy-start.12 = (bf16[8,128,384]{1,2,0:T(8,128)(2,1)S(1)}, bf16[8,128,384]{1,2,0:T(8,128)(2,1)}, u32[]{:S(2)}) copy-start(bf16[8,128,384]{1,2,0:T(8,128)(2,1)} %copy-done.11) | copy-start | bytes 2359300
  633.6 12.5 %all-to-all-start.7 = ((bf16[8,128,384]{2,1,0:T(8,128)(2,1)}), bf16[8,128,384]{2,1,0:T(8,128)(2,1)S(1)}, u32[]{:S(2)}, u32[]{:S(2)}) async-start(bf16[8,128,384]{2,1,0:T(8,128)(2,1)} %copy.95), calls=%async_computation.7 | async-start | bytes 1572864 | tf_op jit(solution)/shard_map/all_to_all | solution.py:183
  (120 other events, 242.7 us)
where the time goes:
time: 651 us; the launch traced here: 648 us
  matrix products  301 us (46%)
  local copies, waits for them, and re-layouts  135 us (21%)
  waiting for transfers between devices  107 us (16%)
  starting transfers between devices  48.4 us (7%)
  other arithmetic  30 us (5%)
  loops' own time  25.1 us (4%)
    dot_general x24, matrix products, spread_tiles(): jnp.einsum('tp,tkhd->pkhd', chooser, values, precision=lax.Precision.HIGH...  103 us
    dot_general x60, matrix products, pick_tiles(): jnp.einsum('tp,pkhd->tkhd', chooser, pool, preferred_element_type=jnp.flo...  94.9 us
    while x300, local copies, waits for them, and re-layouts  48.6 us
    dot_general x12, matrix products, value_pass(): jnp.einsum('thqk,tkhd->tqhd', prob_b, pick_tiles(values_pool, picked), pr...  48 us
    all_to_all x1, waiting for transfers between devices, per_device(): lax.all_to_all(query, 'head', split_axis=1, concat_axis=0, tiled=True)  39.9 us
    dot_general x24, matrix products, tile_scores(): jnp.einsum('tqhd,tkhd->thqk', query_tiles, key_tiles, preferred_element_t...  31.6 us
    convert_element_type x12, local copies, waits for them, and re-layouts, pick_tiles(): return picked.astype(pool.dtype)  28.9 us
    all_to_all x1, waiting for transfers between devices, per_device(): lax.all_to_all(attn_heads, 'head', split_axis=0, concat_axis=1, tiled=True)  25.4 us
  transfers between devices with their start and end apart: 12, of which 8 were waited for; matrix products, arithmetic and copies ran while one was open for 4% of the time, Pallas kernels for 0%

commit v1 on v0

--- a/solution.py
+++ b/solution.py
@@ -77,7 +77,12 @@
     scaling = HD ** (-0.5)
     slab_index = lax.axis_index("seq")
     query_heads, key_heads, value_heads, cotangent_heads = (
-        lax.all_to_all(query, "head", split_axis=1, concat_axis=0, tiled=True),
+        jnp.concatenate(
+            lax.all_to_all(
+                jnp.stack(jnp.split(query, lax.axis_size("head"), axis=1)), "head", 0, 0
+            ),
+            axis=0,
+        ),
         lax.all_to_all(key, "head", split_axis=1, concat_axis=0, tiled=True),
         lax.all_to_all(value, "head", split_axis=1, concat_axis=0, tiled=True),
         lax.all_to_all(grad_out, "head", split_axis=1, concat_axis=0, tiled=True),

time: 651 us -> 643 us (0.988)
  waiting for transfers between devices: 107 us -> 93.6 us
    all_to_all x1, waiting for transfers between devices: 6.62 us -> 0.01 us  [per_device(): lax.all_to_all(grad_out, 'head', split_axis=1, concat_axis=0, tiled=True)]
    unnamed x35 -> x41, local copies, waits for them, and re-layouts: 16.4 us -> 22.6 us
  transfers between devices with their start and end apart: 12 -> 12, of which waited for: 8 -> 7; matrix products, arithmetic and copies ran while one was open for 4% -> 5% of each run, Pallas kernels for 0% -> 0%
where the time goes in v1:
time: 643 us; the launch traced here: 640 us
  matrix products  301 us (47%)
  local copies, waits for them, and re-layouts  139 us (22%)
  waiting for transfers between devices  93.6 us (15%)
  starting transfers between devices  49.4 us (8%)
  other arithmetic  29.5 us (5%)
  loops' own time  25.9 us (4%)
    dot_general x24, matrix products, spread_tiles(): jnp.einsum('tp,tkhd->pkhd', chooser, values, precision=lax.Precision.HIGH...  103 us
    dot_general x60, matrix products, pick_tiles(): jnp.einsum('tp,pkhd->tkhd', chooser, pool, preferred_element_type=jnp.flo...  94.8 us
    while x300, local copies, waits for them, and re-layouts  48.6 us
    dot_general x12, matrix products, value_pass(): jnp.einsum('thqk,tkhd->tqhd', prob_b, pick_tiles(values_pool, picked), pr...  47.9 us
    all_to_all x1, waiting for transfers between devices, per_device(): lax.all_to_all(jnp.stack(jnp.split(query, lax.axis_size('head'), axis=1))...  34.2 us
    dot_general x24, matrix products, tile_scores(): jnp.einsum('tqhd,tkhd->thqk', query_tiles, key_tiles, preferred_element_t...  31.6 us
    convert_element_type x12, local copies, waits for them, and re-layouts, pick_tiles(): return picked.astype(pool.dtype)  28.9 us
    all_to_all x1, waiting for transfers between devices, per_device(): lax.all_to_all(attn_heads, 'head', split_axis=0, concat_axis=1, tiled=True)  25.3 us
  transfers between devices with their start and end apart: 12, of which 7 were waited for; matrix products, arithmetic and copies ran while one was open for 5% of the time, Pallas kernels for 0%

profile of v1, /device:TPU:1, one launch (start us, length us, event | category | flops | bytes accessed | tf_op | source)
XLA Modules:
  0.0 639.6 jit_solution(202515376748436058)
XLA Ops:
  3.3 5.9 all-to-all-start
  11.7 9.2 %all-to-all-done = bf16[128,8,384]{2,0,1:T(8,128)(2,1)S(1)} async-done(((bf16[128,8,384]{2,0,1:T(8,128)(2,1)}), bf16[128,8,384]{2,0,1:T(8,128)(2,1)S(1)}, u32[]{:S(2)}, u32[]{:S(2)}) %all-to-all-start) | async-done | bytes 786464 | tf_op jit(solution)/shard_map/all_to_all | solution.py:86
  31.2 4.7 all-to-all-done.1
  41.1 4.8 collective-permute-start.1
  45.9 4.3 collective-permute-start
  53.1 4.7 all-to-all-start.2
  60.5 34.2 %all-to-all-done.2 = bf16[8,128,384]{1,2,0:T(8,128)(2,1)S(1)} async-done(((bf16[8,128,384]{1,2,0:T(8,128)(2,1)}), bf16[8,128,384]{1,2,0:T(8,128)(2,1)S(1)}, u32[]{:S(2)}, u32[]{:S(2)}) %all-to-all-start.2) | async-done | bytes 786464 | tf_op jit(solution)/shard_map/all_to_all | solution.py:81
  104.7 28.6 %while.36 = (s32[]{:T(128)}, f32[8,3,128]{2,1,0:T(4,128)S(1)}, f32[8,3,128]{2,1,0:T(4,128)S(1)}, s32[]{:T(128)}, s32[8]{0:T(128)S(1)}, /*index=5*/s32[8,12]{0,1:...) while((s32[]{:T(128)}, f32[8,3,128]{2,1,0:T(4,128)S(1)}, ...), condition=%wide.region_4.5_spmd, body=%wide.region_1.4_spmd.sunk | while | flops 121516232 | bytes 8024375 | solution.py:115
  137.0 4.7 copy.100
  143.0 96.4 %while.37 = (s32[]{:T(128)}, f32[8,128,3,128]{1,3,2,0:T(8,128)}, s32[]{:T(128)}, s32[8,12]{0,1:T(8,128)S(1)}, bf16[24,128,3,128]{3,0,2,1:T(8,128)(2,1)}, /*index...) while((s32[]{:T(128)}, f32[8,128,3,128]{1,3,2,0:T(8,128)}, ...), condition=%wide.region_6.7_spmd, body=%wide.region_5.6_spmd.sunk | while | flops 241828240 | bytes 21246324 | solution.py:135
  163.0 4.0 bitcast_add_fusion.4
  170.9 4.0 bitcast_add_fusion.4
  178.9 4.0 bitcast_add_fusion.4
  186.9 4.0 bitcast_add_fusion.4
  194.9 4.0 bitcast_add_fusion.4
  249.7 285.5 %while.38 = (s32[]{:T(128)}, f32[8,128,3,128]{1,3,2,0:T(8,128)}, f32[24,128,3,128]{3,0,2,1:T(8,128)}, f32[24,128,3,128]{3,0,2,1:T(8,128)}, s32[]{:T(128)}, /*ind...) while((s32[]{:T(128)}, f32[8,128,3,128]{1,3,2,0:T(8,128)}, ...), condition=%wide.region_9.10_spmd, body=%wide.region_8.9_spmd.sunk | while | flops 773849856 | bytes 136864496 | solution.py:169
  262.7 4.3 convolution_add_fusion.4
  267.1 4.3 convolution_add_fusion.5
  286.4 4.3 convolution_add_fusion.4
  290.8 4.3 convolution_add_fusion.5
  310.1 4.3 convolution_add_fusion.4
  314.5 4.3 convolution_add_fusion.5
  333.9 4.3 convolution_add_fusion.4
  338.2 4.3 convolution_add_fusion.5
  357.6 4.3 convolution_add_fusion.4
  361.9 4.3 convolution_add_fusion.5
  381.3 4.3 convolution_add_fusion.4
  385.6 4.3 convolution_add_fusion.5
  405.0 4.3 convolution_add_fusion.4
  409.4 4.3 convolution_add_fusion.5
  428.7 4.3 convolution_add_fusion.4
  433.1 4.3 convolution_add_fusion.5
  452.4 4.3 convolution_add_fusion.4
  456.8 4.3 convolution_add_fusion.5
  476.1 4.3 convolution_add_fusion.4
  480.5 4.3 convolution_add_fusion.5
  499.9 4.3 convolution_add_fusion.4
  504.2 4.3 convolution_add_fusion.5
  523.6 4.3 convolution_add_fusion.4
  527.9 4.3 convolution_add_fusion.5
  535.2 6.0 copy.112
  544.0 6.1 copy.110
  557.7 5.3 collective-permute-start.2
  568.0 25.3 %all-to-all-done.3 = bf16[8,128,384]{1,2,0:T(8,128)(2,1)S(1)} async-done(((bf16[8,128,384]{1,2,0:T(8,128)(2,1)}), bf16[8,128,384]{1,2,0:T(8,128)(2,1)S(1)}, u32[]{:S(2)}, u32[]{:S(2)}) %all-to-all-start.3) | async-done | bytes 786464 | tf_op jit(solution)/shard_map/all_to_all | solution.py:139
  593.3 4.4 all-to-all-start.5
  605.3 5.1 all-to-all-done.5
  615.1 10.3 %all-to-all-done.6 = bf16[8,128,384]{2,1,0:T(8,128)(2,1)S(1)} async-done(((bf16[8,128,384]{2,1,0:T(8,128)(2,1)}), bf16[8,128,384]{2,1,0:T(8,128)(2,1)S(1)}, u32[]{:S(2)}, u32[]{:S(2)}) %all-to-all-start.6) | async-done | bytes 786464 | tf_op jit(solution)/shard_map/all_to_all | solution.py:187
  633.3 4.7 all-to-all-done.7
  (672 shorter events, 349.5 us)
Async XLA Ops:
  2.1 7.1 %copy-start.12 = (bf16[128,3072]{1,0:T(8,128)(2,1)S(1)}, bf16[128,3072]{1,0:T(8,128)(2,1)}, u32[]{:S(2)}) copy-start(bf16[128,3072]{1,0:T(8,128)(2,1)} %param.14) | copy-start | bytes 2359300
  3.3 17.6 %all-to-all-start = ((bf16[128,8,384]{2,0,1:T(8,128)(2,1)}), bf16[128,8,384]{2,0,1:T(8,128)(2,1)S(1)}, u32[]{:S(2)}, u32[]{:S(2)}) async-start(bf16[128,8,384]{2,0,1:T(8,128)(2,1)} %copy.85), calls=%async_computation | async-start | bytes 1572864 | tf_op jit(solution)/shard_map/all_to_all | solution.py:86
  10.8 13.9 %copy-start.14 = (bf16[128,3072]{1,0:T(8,128)(2,1)S(1)}, bf16[128,3072]{1,0:T(8,128)(2,1)}, u32[]{:S(2)}) copy-start(bf16[128,3072]{1,0:T(8,128)(2,1)} %param.15) | copy-start | bytes 2359300
  20.9 15.0 %all-to-all-start.1 = ((bf16[128,8,384]{2,0,1:T(8,128)(2,1)}), bf16[128,8,384]{2,0,1:T(8,128)(2,1)S(1)}, u32[]{:S(2)}, u32[]{:S(2)}) async-start(bf16[128,8,384]{2,0,1:T(8,128)(2,1)} %copy.87), calls=%async_computation.1 | async-start | bytes 1572864 | tf_op jit(solution)/shard_map/all_to_all | solution.py:87
  35.9 17.2 %all-to-all-start.4 = ((bf16[128,8,384]{0,2,1:T(8,128)(2,1)}), bf16[128,8,384]{0,2,1:T(8,128)(2,1)S(1)}, u32[]{:S(2)}, u32[]{:S(2)}) async-start(bf16[128,8,384]{0,2,1:T(8,128)(2,1)} %bitcast.34), calls=%async_computation.4 | async-start | bytes 1572864 | tf_op jit(solution)/shard_map/all_to_all | solution.py:88
  41.1 18.2 %copy-start.15 = (s32[256,12]{0,1:T(8,128)S(1)}, s32[256,12]{0,1:T(8,128)}, u32[]{:S(2)}) copy-start(s32[256,12]{0,1:T(8,128)} %param.16) | copy-start | bytes 36868
  41.1 54.1 %collective-permute-start.1 = (bf16[2,1024,384]{1,2,0:T(8,128)(2,1)}, bf16[2,1024,384]{1,2,0:T(8,128)(2,1)}, u32[]{:S(2)}, u32[]{:S(2)}) collective-permute-start(bf16[2,1024,384]{1,2,0:T(8,128)(2,1)} %pad_maximum_fusion.1), channel_id=1, source_target_pairs={{1,0},{2,1},{3,2},{4,3},{5,4},{6,5},{7,6},{8,7},{9,8},{10,9},{11,1... | collective-permute-start | bytes 4718600 | tf_op jit(solution)/shard_map/ppermute | solution.py:22
  45.9 49.3 %collective-permute-start = (bf16[2,1024,384]{1,2,0:T(8,128)(2,1)}, bf16[2,1024,384]{1,2,0:T(8,128)(2,1)}, u32[]{:S(2)}, u32[]{:S(2)}) collective-permute-start(bf16[2,1024,384]{1,2,0:T(8,128)(2,1)} %pad_maximum_fusion.1), channel_id=1, source_target_pairs={{0,1},{1,2},{2,3},{3,4},{4,5},{5,6},{6,7},{7,8},{8,9},{9,10},{10,1... | collective-permute-start | bytes 4718600 | tf_op jit(solution)/shard_map/ppermute | solution.py:20
  53.1 7.4 %copy-start.9 = (bf16[128,8,384]{0,2,1:T(8,128)(2,1)}, bf16[128,8,384]{0,2,1:T(8,128)(2,1)S(1)}, u32[]{:S(2)}) copy-start(bf16[128,8,384]{0,2,1:T(8,128)(2,1)S(1)} %all-to-all-done.4) | copy-start | bytes 2359300
  53.1 41.6 %all-to-all-start.2 = ((bf16[8,128,384]{1,2,0:T(8,128)(2,1)}), bf16[8,128,384]{1,2,0:T(8,128)(2,1)S(1)}, u32[]{:S(2)}, u32[]{:S(2)}) async-start(bf16[8,128,384]{1,2,0:T(8,128)(2,1)} %bitcast_dynamic-update-slice_fusion), calls=%async_computation.2 | async-start | bytes 1572864 | tf_op jit(solution)/shard_map/all_to_all | solution.py:81
  261.5 5.5 slice-start
  262.7 4.3 slice-start.1
  285.3 5.5 slice-start
  286.4 4.3 slice-start.1
  290.8 4.3 copy-start.2
  309.0 5.5 slice-start
  310.1 4.3 slice-start.1
  332.7 5.5 slice-start
  333.9 4.3 slice-start.1
  338.2 4.3 copy-start.2
  356.4 5.5 slice-start
  357.6 4.3 slice-start.1
  361.9 4.3 copy-start.2
  380.1 5.5 slice-start
  381.3 4.3 slice-start.1
  385.6 4.3 copy-start.2
  403.8 5.5 slice-start
  405.0 4.3 slice-start.1
  409.3 4.3 copy-start.2
  427.5 5.5 slice-start
  428.7 4.3 slice-start.1
  433.1 4.3 copy-start.2
  451.3 5.5 slice-start
  452.4 4.3 slice-start.1
  456.8 4.3 copy-start.2
  475.0 5.5 slice-start
  476.1 4.3 slice-start.1
  498.7 5.5 slice-start
  499.9 4.3 slice-start.1
  522.4 5.5 slice-start
  523.6 4.3 slice-start.1
  554.5 43.2 %collective-permute-start.3 = (bf16[2,8,128,3,128]{2,4,3,1,0:T(8,128)(2,1)}, bf16[2,8,128,3,128]{2,4,3,1,0:T(8,128)(2,1)}, u32[]{:S(2)}, u32[]{:S(2)}) collective-permute-start(bf16[2,8,128,3,128]{2,4,3,1,0:T(8,128)(2,1)} %pad_maximum_fusion.3), channel_id=1, source_target_pairs={{1,0},{2,1},{3,2},{4,3},{5,4},{6,5},{7,6},{8,7},{9,8},{10,9},{11,1... | collective-permute-start | bytes 4718600 | tf_op jit(solution)/shard_map/ppermute | solution.py:32
  557.7 8.8 %copy-start.8 = (f32[8,128,3,128]{1,3,2,0:T(8,128)S(1)}, f32[8,128,3,128]{1,3,2,0:T(8,128)}, u32[]{:S(2)}) copy-start(f32[8,128,3,128]{1,3,2,0:T(8,128)} %get-tuple-element.169) | copy-start | bytes 4718596
  557.7 41.8 %collective-permute-start.2 = (bf16[2,8,128,3,128]{2,4,3,1,0:T(8,128)(2,1)}, bf16[2,8,128,3,128]{2,4,3,1,0:T(8,128)(2,1)}, u32[]{:S(2)}, u32[]{:S(2)}) collective-permute-start(bf16[2,8,128,3,128]{2,4,3,1,0:T(8,128)(2,1)} %pad_maximum_fusion.2), channel_id=1, source_target_pairs={{0,1},{1,2},{2,3},{3,4},{4,5},{5,6},{6,7},{7,8},{8,9},{9,10},{10,1... | collective-permute-start | bytes 4718600 | tf_op jit(solution)/shard_map/ppermute | solution.py:32
  563.0 30.3 %all-to-all-start.3 = ((bf16[8,128,384]{1,2,0:T(8,128)(2,1)}), bf16[8,128,384]{1,2,0:T(8,128)(2,1)S(1)}, u32[]{:S(2)}, u32[]{:S(2)}) async-start(bf16[8,128,384]{1,2,0:T(8,128)(2,1)} %bitcast.31), calls=%async_computation.3 | async-start | bytes 1572864 | tf_op jit(solution)/shard_map/all_to_all | solution.py:139
  593.3 17.1 %all-to-all-start.5 = ((bf16[8,128,384]{2,1,0:T(8,128)(2,1)}), bf16[8,128,384]{2,1,0:T(8,128)(2,1)S(1)}, u32[]{:S(2)}, u32[]{:S(2)}) async-start(bf16[8,128,384]{2,1,0:T(8,128)(2,1)} %copy.108), calls=%async_computation.5 | async-start | bytes 1572864 | tf_op jit(solution)/shard_map/all_to_all | solution.py:186
  610.4 15.0 %all-to-all-start.6 = ((bf16[8,128,384]{2,1,0:T(8,128)(2,1)}), bf16[8,128,384]{2,1,0:T(8,128)(2,1)S(1)}, u32[]{:S(2)}, u32[]{:S(2)}) async-start(bf16[8,128,384]{2,1,0:T(8,128)(2,1)} %copy.113), calls=%async_computation.6 | async-start | bytes 1572864 | tf_op jit(solution)/shard_map/all_to_all | solution.py:187
  625.4 12.6 %all-to-all-start.7 = ((bf16[8,128,384]{2,1,0:T(8,128)(2,1)}), bf16[8,128,384]{2,1,0:T(8,128)(2,1)S(1)}, u32[]{:S(2)}, u32[]{:S(2)}) async-start(bf16[8,128,384]{2,1,0:T(8,128)(2,1)} %copy.116), calls=%async_computation.7 | async-start | bytes 1572864 | tf_op jit(solution)/shard_map/all_to_all | solution.py:188
  (116 other events, 222.1 us)
